TPU v7x, 32 devices: a whole 2x2x4 slice. The times are simulated.
32 devices in a mesh: dp: 4 (over y, core), item: 8 (over z, x).
Axes of the slice: x: 2, y: 2, z: 4, core: 2. Of those that a mesh axis runs over, the one named last changes fastest.
Arguments:
- query: bfloat16 [32, 256], P(('dp', 'item')), may hold values from -40 to 40
- item_table: bfloat16 [65536, 256], P(('dp', 'item')), may hold values from -2.5 to 2.5
- context_features: bfloat16 [32, 512], P(('dp', 'item')), may hold values from -6 to 6
- candidates: int32 [32, 1024], P(('dp', 'item')), may hold values from 0 to 65535, as said below
- lengths: int32 [32], P(('dp', 'item')), may hold values from 128 to 1024, as said below
- logged_slot: int32 [32], P(('dp', 'item')), may hold values from 0 to 1023, as said below
- logging_prop: int32 [32], P(('dp', 'item')), may hold values from 256 to 4095
- w_first: bfloat16 [768, 512], replicated, may hold values from -0.21875 to 0.21875
- w_second: bfloat16 [512, 512], replicated, may hold values from -0.25 to 0.25
- w_score: bfloat16 [512], replicated, may hold values from -0.5 to 0.5
Outputs:
- section_logp: float32 [32, 1024], P(('dp', 'item'))
- log_weight: float32 [32], P(('dp', 'item'))
Inputs may be any that keep to these rules, and one draw needn't show every extreme that they name: `candidates`: item ids. Among the 1024 candidate slots held by one device (its single context), at most 48 name items of any one block of 2048 consecutive ids, and for every device some block is named exactly 48 times. `lengths`: some context's list has 1024 live slots and some context's list has 128. `logged_slot`: below the context's length; the context with the longest list logs its last slot.
All inputs are finite; a program needn't handle non-finite values.
Results may differ from a plain program's by a relative error of at most 0.0003.
Values may be sent and summed in bfloat16 or wider, within the bound.
A program may use at most 64 MiB of HBM per device.

v0:
```python
import math
import jax
import jax.numpy as jnp
from jax import lax
from jax.sharding import PartitionSpec as P


def merged(array, axis, combine):
    everything = jax.tree.map(lambda part: lax.all_gather(part, axis), array)
    leading = jax.tree.map(lambda part: part[0], everything)

    def step(k, so_far):
        return combine(so_far, jax.tree.map(lambda part: part[k], everything))

    return lax.fori_loop(1, lax.axis_size(axis), step, leading)


def combine_pairs(earlier, later):
    new_max = jnp.maximum(earlier[0], later[0])
    new_sum = earlier[1] * jnp.exp(earlier[0] - new_max) + later[1] * jnp.exp(later[0] - new_max)
    return (new_max, new_sum)


def body(
    query,
    item_table,
    context_features,
    candidates,
    lengths,
    logged_slot,
    logging_prop,
    w_first,
    w_second,
    w_score,
):
    device_count = lax.axis_size("dp") * lax.axis_size("item")
    item_rows = item_table.shape[0]
    width = item_table.shape[1]
    own_count = query.shape[0]
    slot_count = candidates.shape[1]
    gathered = lax.all_gather(query, ("dp", "item"), axis=0, tiled=True)
    context_total = gathered.shape[0]
    block_rows = min(512, item_rows)
    slabs = item_table.reshape(item_rows // block_rows, block_rows, width)

    def sweep(running, slab_rows):
        running_max, running_sum = running
        logits = lax.dot_general(
            gathered, slab_rows, (((1,), (1,)), ((), ())), preferred_element_type=jnp.float32
        )
        new_max = jnp.maximum(running_max, jnp.max(logits, axis=1))
        new_sum = running_sum * jnp.exp(running_max - new_max) + jnp.sum(
            jnp.exp(logits - new_max[:, None]), axis=1
        )
        return ((new_max, new_sum), None)

    initial = (
        jnp.full((context_total,), -1e30, jnp.float32),
        jnp.zeros((context_total,), jnp.float32),
    )
    (local_max, local_sum), unused_out = lax.scan(sweep, initial, slabs)
    first_context = lax.axis_index(("dp", "item")) * own_count
    global_max, global_sum = merged((local_max, local_sum), ("dp", "item"), combine_pairs)
    log_norm = lax.dynamic_slice_in_dim(global_max + jnp.log(global_sum), first_context, own_count)
    capacity = max(2, 3 * own_count * slot_count // (2 * device_count))
    flat_ids = candidates.reshape(-1)
    holder = flat_ids // item_rows
    same_holder = holder[:, None] == holder[None, :]
    earlier_slot = jnp.arange(flat_ids.shape[0])[None, :] < jnp.arange(flat_ids.shape[0])[:, None]
    holder_rank = jnp.sum((same_holder & earlier_slot).astype(jnp.int32), axis=1)
    bucket = holder * capacity + holder_rank
    outgoing = jnp.full((device_count * capacity,), -1, jnp.int32).at[bucket].set(flat_ids)
    outgoing = outgoing.reshape(lax.axis_size("dp"), lax.axis_size("item"), capacity)
    first_item = lax.axis_index(("dp", "item")) * item_rows
    asked_ids = lax.all_to_all(
        lax.all_to_all(outgoing, "dp", split_axis=0, concat_axis=0, tiled=True),
        "item",
        split_axis=1,
        concat_axis=1,
        tiled=True,
    )
    local_index = jnp.clip(asked_ids - first_item, 0, item_rows - 1)
    fetched = lax.all_to_all(
        lax.all_to_all(item_table[local_index], "dp", split_axis=0, concat_axis=0, tiled=True),
        "item",
        split_axis=1,
        concat_axis=1,
        tiled=True,
    )
    cand_rows = fetched.reshape(device_count * capacity, width)[bucket]
    rows_by_context = cand_rows.reshape(own_count, slot_count, width)
    gen_logit = jnp.einsum("cd,ckd->ck", query, rows_by_context, preferred_element_type=jnp.float32)
    feature_width = context_features.shape[1]
    context_part = jnp.dot(
        context_features, w_first[:feature_width], preferred_element_type=jnp.float32
    )
    item_part = jnp.dot(cand_rows, w_first[feature_width:], preferred_element_type=jnp.float32)
    item_part = item_part.reshape(own_count, slot_count, -1)
    hidden = jax.nn.silu(item_part + context_part[:, None, :]).astype(jnp.bfloat16)
    hidden = hidden.reshape(own_count * slot_count, -1)
    second = jax.nn.silu(jnp.dot(hidden, w_second, preferred_element_type=jnp.float32)).astype(
        jnp.bfloat16
    )
    score = jnp.dot(second, w_score, preferred_element_type=jnp.float32).reshape(
        own_count, slot_count
    )
    positions = jnp.arange(slot_count, dtype=jnp.int32)
    live_slots = positions[None, :] < lengths[:, None]
    masked = jnp.where(live_slots, score, jnp.float32(-1e30))
    rank_peak = jnp.max(masked, axis=1)
    rank_norm = rank_peak + jnp.log(
        jnp.sum(
            jnp.where(live_slots, jnp.exp(masked - rank_peak[:, None]), jnp.float32(0.0)), axis=1
        )
    )
    total_items = item_rows * device_count
    section = jnp.where(
        live_slots,
        score - rank_norm[:, None] + gen_logit - log_norm[:, None] + math.log(total_items),
        jnp.float32(0.0),
    )
    chosen = jnp.sum(
        jnp.where(positions[None, :] == logged_slot[:, None], section, jnp.float32(0.0)), axis=1
    )
    log_weight = (
        chosen
        + jnp.log(lengths.astype(jnp.float32))
        - jnp.log(logging_prop.astype(jnp.float32) / 1024.0)
    )
    return (section, log_weight)


def solution(mesh):
    in_specs = (
        P(("dp", "item"), None),
        P(("dp", "item"), None),
        P(("dp", "item"), None),
        P(("dp", "item"), None),
        P(("dp", "item")),
        P(("dp", "item")),
        P(("dp", "item")),
        P(),
        P(),
        P(),
    )
    out_specs = (P(("dp", "item"), None), P(("dp", "item")))
    return jax.shard_map(body, mesh=mesh, in_specs=in_specs, out_specs=out_specs, check_vma=False)
```

profile of v0, /device:TPU:0, one launch (start us, length us, event | category | flops | bytes accessed | tf_op | source)
XLA Modules:
  0.0 184.3 jit_solution(8159638173040724396)
XLA Ops:
  0.6 0.8 and_select_fusion
  1.4 0.7 add_select_fusion
  2.6 0.7 compare_select_fusion.1
  3.4 4.5 %scatter_custom_fusion = s32[1536]{0:T(1024)S(1)} fusion(s32[1024]{0:T(1024)S(1)} %bitcast.83, s32[1024]{0:T(1024)} %bitcast.81, s32[]{:T(128)} %constant.87.clone.1), kind=kCustom, calls=%fused_computation.53 | custom fusion | bytes 6656 | tf_op jit(solution)/shard_map/scatter | solution.py:72
  8.0 7.9 %all_to_all.20 = s32[4,1,384]{2,1,0:T(1,128)S(1)} all-to-all(s32[4,1,384]{2,1,0:T(1,128)S(1)} %reshape.234), channel_id=1, replica_groups=mesh['dp'=4,'item'=8] {'dp'}, dimensions={0} | all-to-all | bytes 12288 | tf_op jit(solution)/shard_map/all_to_all | solution.py:76
  17.2 0.7 reshape.236
  17.8 5.8 %all-to-all-start.1 = ((s32[8,1,192]{2,1,0:T(1,128)}), s32[8,1,192]{2,1,0:T(1,128)S(1)}, u32[]{:S(2)}, u32[]{:S(2)}) async-start(s32[8,1,192]{2,1,0:T(1,128)} %reshape.236), calls=%async_computation.1 | async-start | bytes 16384 | tf_op jit(solution)/shard_map/all_to_all | solution.py:75
  23.7 66.8 %all-gather.2 = bf16[32,1,256]{2,1,0:T(2,128)(2,1)S(1)} all-gather(bf16[1,1,256]{2,1,0:T(2,128)(2,1)} %bitcast.85), channel_id=1, replica_groups=mesh['dp'=4,'item'=8] {'dp','item'}, dimensions={0}, use_global_device_ids=true | all-gather | bytes 16896 | tf_op jit(solution)/shard_map/all_gather | solution.py:41
  91.3 5.9 %gather_fusion = bf16[1536,256]{1,0:T(8,128)(2,1)} fusion(bf16[2048,256]{1,0:T(8,128)(2,1)} %param.15, s32[2048]{0:T(1024)S(1)} %pad_clamp_fusion), kind=kCustom, calls=%fused_computation | custom fusion | bytes 1579008 | tf_op jit(solution)/shard_map/gather | solution.py:84
  97.2 3.5 %all-to-all-start.2 = ((bf16[4,8,48,256]{3,2,1,0:T(8,128)(2,1)}), bf16[4,8,48,256]{3,2,1,0:T(8,128)(2,1)S(1)}, u32[]{:S(2)}, u32[]{:S(2)}) async-start(bf16[4,8,48,256]{3,2,1,0:T(8,128)(2,1)} %bitcast.8), calls=%async_computation.2 | async-start | bytes 1572864 | tf_op jit(solution)/shard_map/all_to_all | solution.py:84
  100.7 6.0 %while.31 = (s32[]{:T(128)}, f32[32]{0:T(128)S(1)}, f32[32]{0:T(128)S(1)}, bf16[4,512,256]{2,1,0:T(8,128)(2,1)}, bf16[32,256]{1,0:T(8,128)(2,1)S(1)}, /*index=5*/s32[]{:T(128)}, s32[]{:T(128)}) while((s32[]{:T(128)}, f32[32]{0:T(128)S(1)}, f32[32]{0:T(128)S(1)}, bf16[4,512,256]{2,1,0:T(8,128)(2,1)}, bf16[32,256]{1,0:T(8,128)(2,1)S(1)}, ...), condition=%wide.region_7.8_spmd.clone, body=%wide.region_4.7_spmd.clone.sunk | while | flops 8437923 | bytes 411864 | solution.py:61
  100.7 1.2 fusion.42
  102.2 1.2 fusion.42
  103.7 1.2 fusion.42
  105.2 1.2 fusion.42
  107.2 37.0 %all-reduce.2 = (f32[1024]{0:T(1024)S(1)}, f32[1024]{0:T(1024)S(1)}) all-reduce(f32[1024]{0:T(1024)S(1)} %dynamic-update-slice, f32[1024]{0:T(1024)S(1)} %dynamic-update-slice.1), channel_id=2, replica_groups=mesh['dp'=4,'item'=8] {'dp','item'}, use_global_device_ids=true, to_apply=%add | all-reduce | flops 2048 | bytes 16384
  144.3 1.0 copy.24
  145.2 6.1 %all-to-all-start.3 = ((bf16[4,8,48,256]{3,2,0,1:T(8,128)(2,1)}), bf16[4,8,48,256]{3,2,0,1:T(8,128)(2,1)S(1)}, u32[]{:S(2)}, u32[]{:S(2)}) async-start(bf16[4,8,48,256]{3,2,0,1:T(8,128)(2,1)} %copy.24), calls=%async_computation.3 | async-start | bytes 1572864 | tf_op jit(solution)/shard_map/all_to_all | solution.py:83
  151.3 1.4 while.30
  155.6 15.6 %all-to-all-done.3 = bf16[4,8,48,256]{3,2,0,1:T(8,128)(2,1)S(1)} async-done(((bf16[4,8,48,256]{3,2,0,1:T(8,128)(2,1)}), bf16[4,8,48,256]{3,2,0,1:T(8,128)(2,1)S(1)}, u32[]{:S(2)}, u32[]{:S(2)}) %all-to-all-start.3) | async-done | bytes 786464 | tf_op jit(solution)/shard_map/all_to_all | solution.py:83
  171.3 3.9 %gather_fusion.1 = bf16[1024,256]{1,0:T(8,128)(2,1)S(1)} fusion(bf16[1536,256]{1,0:T(8,128)(2,1)S(1)} %bitcast.74, s32[1024]{0:T(1024)S(1)} %broadcast_clamp_fusion), kind=kCustom, calls=%fused_computation.1 | custom fusion | bytes 1052672 | tf_op jit(solution)/shard_map/gather | solution.py:90
  175.5 1.4 multiply_convert_fusion
  177.9 1.3 select_reduce_fusion.1
  180.6 1.9 %select_reduce_fusion = (f32[]{:T(128)}, f32[1024]{0:T(1024)}) fusion(s32[]{:T(128)} %bitcast.72, f32[]{:T(128)} %bitcast.15, f32[1024]{0:T(1024)S(1)} %bitcast.82, f32[1024]{0:T(1024)S(1)} %bitcast.78, f32[]{:T(128)S(6)} %add.144, s32[]{:T(128)} %bitcast.71), kind=kLoop, calls=%fused_computation.48 | loop fusion | flops 9215 | bytes 12308 | tf_op jit(solution)/shard_map/reduce_sum | solution.py:122
  (92 shorter events, 7.3 us)
Async XLA Ops:
  0.6 174.8 %copy-start = (bf16[512,512]{1,0:T(8,128)(2,1)S(1)}, bf16[512,512]{1,0:T(8,128)(2,1)}, u32[]{:S(2)}) copy-start(bf16[512,512]{1,0:T(8,128)(2,1)} %param.22) | copy-start | bytes 1572868
  17.8 72.6 %all-to-all-start.1 = ((s32[8,1,192]{2,1,0:T(1,128)}), s32[8,1,192]{2,1,0:T(1,128)S(1)}, u32[]{:S(2)}, u32[]{:S(2)}) async-start(s32[8,1,192]{2,1,0:T(1,128)} %reshape.236), calls=%async_computation.1 | async-start | bytes 16384 | tf_op jit(solution)/shard_map/all_to_all | solution.py:75
  97.2 47.1 %all-to-all-start.2 = ((bf16[4,8,48,256]{3,2,1,0:T(8,128)(2,1)}), bf16[4,8,48,256]{3,2,1,0:T(8,128)(2,1)S(1)}, u32[]{:S(2)}, u32[]{:S(2)}) async-start(bf16[4,8,48,256]{3,2,1,0:T(8,128)(2,1)} %bitcast.8), calls=%async_computation.2 | async-start | bytes 1572864 | tf_op jit(solution)/shard_map/all_to_all | solution.py:84
  145.2 7.5 %copy-start.4 = (bf16[512]{0:T(512)(128)(2,1)S(1)}, bf16[512]{0:T(512)(128)(2,1)}, u32[]{:S(2)}) copy-start(bf16[512]{0:T(512)(128)(2,1)} %param.23) | copy-start | bytes 3076
  145.2 10.2 %copy-start.1 = (bf16[768,512]{1,0:T(8,128)(2,1)S(1)}, bf16[768,512]{1,0:T(8,128)(2,1)}, u32[]{:S(2)}) copy-start(bf16[768,512]{1,0:T(8,128)(2,1)} %param.21) | copy-start | bytes 2359300
  145.2 10.2 %copy-start.3 = (bf16[1,512]{1,0:T(2,128)(2,1)S(1)}, bf16[1,512]{1,0:T(2,128)(2,1)}, u32[]{:S(2)}) copy-start(bf16[1,512]{1,0:T(2,128)(2,1)} %param.16) | copy-start | bytes 3076
  145.2 25.9 %all-to-all-start.3 = ((bf16[4,8,48,256]{3,2,0,1:T(8,128)(2,1)}), bf16[4,8,48,256]{3,2,0,1:T(8,128)(2,1)S(1)}, u32[]{:S(2)}, u32[]{:S(2)}) async-start(bf16[4,8,48,256]{3,2,0,1:T(8,128)(2,1)} %copy.24), calls=%async_computation.3 | async-start | bytes 1572864 | tf_op jit(solution)/shard_map/all_to_all | solution.py:83
  171.2 4.0 %copy-start.2 = (bf16[1,256]{1,0:T(2,128)(2,1)S(1)}, bf16[1,256]{1,0:T(2,128)(2,1)}, u32[]{:S(2)}) copy-start(bf16[1,256]{1,0:T(2,128)(2,1)} %param.14) | copy-start | bytes 1540
where the time goes:
time: 185 us; the launch traced here: 184 us
  blocking collectives  112 us (61%)
  local copies, waits for them, and re-layouts  18.2 us (10%)
  waiting for transfers between devices  15.6 us (8%)
  starting transfers between devices  15.4 us (8%)
  other arithmetic  9.64 us (5%)
  matrix products  7.17 us (4%)
  between operations  6.05 us (3%)
    all_gather x1, blocking collectives, body(): gathered = lax.all_gather(query, ('dp', 'item'), axis=0, tiled=True)  66.8 us
    unnamed x1, blocking collectives  37 us
    all_to_all x1, waiting for transfers between devices, body(): lax.all_to_all(lax.all_to_all(item_table[local_index], 'dp', split_axis=0...  15.6 us
    all_to_all x1, blocking collectives, body(): lax.all_to_all(outgoing, 'dp', split_axis=0, concat_axis=0, tiled=True)  7.87 us
    all_to_all x1, starting transfers between devices, body(): lax.all_to_all(lax.all_to_all(item_table[local_index], 'dp', split_axis=0...  6.09 us
    gather x1, local copies, waits for them, and re-layouts, body(): item_table[local_index]  5.85 us
    all_to_all x1, starting transfers between devices, body(): lax.all_to_all(lax.all_to_all(outgoing, 'dp', split_axis=0, concat_axis=0...  5.81 us
    dot_general x4, matrix products, sweep(): lax.dot_general(gathered, slab_rows, (((1,), (1,)), ((), ())), preferred_...  4.97 us
  transfers between devices with their start and end apart: 3, of which 1 were waited for; matrix products, arithmetic and copies ran while one was open for 4% of the time, Pallas kernels for 0%

commit v1 on v0

--- a/solution.py
+++ b/solution.py
@@ -80,12 +80,22 @@
         tiled=True,
     )
     local_index = jnp.clip(asked_ids - first_item, 0, item_rows - 1)
-    fetched = lax.all_to_all(
-        lax.all_to_all(item_table[local_index], "dp", split_axis=0, concat_axis=0, tiled=True),
-        "item",
-        split_axis=1,
-        concat_axis=1,
-        tiled=True,
+    fetched = jnp.concatenate(
+        lax.all_to_all(
+            jnp.stack(
+                jnp.split(
+                    lax.all_to_all(
+                        item_table[local_index], "dp", split_axis=0, concat_axis=0, tiled=True
+                    ),
+                    lax.axis_size("item"),
+                    axis=1,
+                )
+            ),
+            "item",
+            0,
+            0,
+        ),
+        axis=1,
     )
     cand_rows = fetched.reshape(device_count * capacity, width)[bucket]
     rows_by_context = cand_rows.reshape(own_count, slot_count, width)

time: 185 us -> 189 us (1.022)
  local copies, waits for them, and re-layouts: 18.2 us -> 22.3 us
    unnamed x18 -> x25, local copies, waits for them, and re-layouts: 1.42 us -> 5.91 us
where the time goes in v1:
time: 189 us; the launch traced here: 188 us
  blocking collectives  112 us (59%)
  local copies, waits for them, and re-layouts  22.3 us (12%)
  waiting for transfers between devices  15.6 us (8%)
  starting transfers between devices  15.3 us (8%)
  other arithmetic  9.64 us (5%)
  matrix products  7.17 us (4%)
  between operations  6.06 us (3%)
    all_gather x1, blocking collectives, body(): gathered = lax.all_gather(query, ('dp', 'item'), axis=0, tiled=True)  66.8 us
    unnamed x1, blocking collectives  37 us
    all_to_all x1, waiting for transfers between devices, body(): lax.all_to_all(jnp.stack(jnp.split(lax.all_to_all(item_table[local_index]...  15.6 us
    all_to_all x1, blocking collectives, body(): lax.all_to_all(outgoing, 'dp', split_axis=0, concat_axis=0, tiled=True)  7.87 us
    all_to_all x1, starting transfers between devices, body(): lax.all_to_all(jnp.stack(jnp.split(lax.all_to_all(item_table[local_index]...  5.96 us
    unnamed x25, local copies, waits for them, and re-layouts  5.91 us
    gather x1, local copies, waits for them, and re-layouts, body(): item_table[local_index]  5.85 us
    all_to_all x1, starting transfers between devices, body(): lax.all_to_all(lax.all_to_all(outgoing, 'dp', split_axis=0, concat_axis=0...  5.81 us
  transfers between devices with their start and end apart: 3, of which 1 were waited for; matrix products, arithmetic and copies ran while one was open for 4% of the time, Pallas kernels for 0%

profile of v1, /device:TPU:0, one launch (start us, length us, event | category | flops | bytes accessed | tf_op | source)
XLA Modules:
  0.0 188.4 jit_solution(11264271317777659092)
XLA Ops:
  0.6 0.8 and_select_fusion
  1.4 0.7 add_select_fusion
  2.6 0.7 compare_select_fusion.1
  3.4 4.5 %scatter_custom_fusion = s32[1536]{0:T(1024)S(1)} fusion(s32[1024]{0:T(1024)S(1)} %bitcast.131, s32[1024]{0:T(1024)} %bitcast.129, s32[]{:T(128)} %constant.87.clone.1), kind=kCustom, calls=%fused_computation.69 | custom fusion | bytes 6656 | tf_op jit(solution)/shard_map/scatter | solution.py:72
  8.0 7.9 %all_to_all.20 = s32[4,1,384]{2,1,0:T(1,128)S(1)} all-to-all(s32[4,1,384]{2,1,0:T(1,128)S(1)} %reshape.234), channel_id=1, replica_groups=mesh['dp'=4,'item'=8] {'dp'}, dimensions={0} | all-to-all | bytes 12288 | tf_op jit(solution)/shard_map/all_to_all | solution.py:76
  17.2 0.7 reshape.236
  17.8 5.8 %all-to-all-start.1 = ((s32[8,1,192]{2,1,0:T(1,128)}), s32[8,1,192]{2,1,0:T(1,128)S(1)}, u32[]{:S(2)}, u32[]{:S(2)}) async-start(s32[8,1,192]{2,1,0:T(1,128)} %reshape.236), calls=%async_computation.1 | async-start | bytes 16384 | tf_op jit(solution)/shard_map/all_to_all | solution.py:75
  23.7 66.8 %all-gather.2 = bf16[32,1,256]{2,1,0:T(2,128)(2,1)S(1)} all-gather(bf16[1,1,256]{2,1,0:T(2,128)(2,1)} %bitcast.133), channel_id=1, replica_groups=mesh['dp'=4,'item'=8] {'dp','item'}, dimensions={0}, use_global_device_ids=true | all-gather | bytes 16896 | tf_op jit(solution)/shard_map/all_gather | solution.py:41
  90.5 0.7 reduce.9
  91.3 5.9 %gather_fusion = bf16[1536,256]{1,0:T(8,128)(2,1)} fusion(bf16[2048,256]{1,0:T(8,128)(2,1)} %param.15, s32[2048]{0:T(1024)S(1)} %pad_clamp_fusion), kind=kCustom, calls=%fused_computation | custom fusion | bytes 1579008 | tf_op jit(solution)/shard_map/gather | solution.py:88
  97.2 3.5 %all-to-all-start.2 = ((bf16[4,8,48,256]{3,2,1,0:T(8,128)(2,1)}), bf16[4,8,48,256]{3,2,1,0:T(8,128)(2,1)S(1)}, u32[]{:S(2)}, u32[]{:S(2)}) async-start(bf16[4,8,48,256]{3,2,1,0:T(8,128)(2,1)} %bitcast.8), calls=%async_computation.2 | async-start | bytes 1572864 | tf_op jit(solution)/shard_map/all_to_all | solution.py:87
  100.7 6.0 %while.31 = (s32[]{:T(128)}, f32[32]{0:T(128)S(1)}, f32[32]{0:T(128)S(1)}, bf16[4,512,256]{2,1,0:T(8,128)(2,1)}, bf16[32,256]{1,0:T(8,128)(2,1)S(1)}, /*index=5*/s32[]{:T(128)}, s32[]{:T(128)}) while((s32[]{:T(128)}, f32[32]{0:T(128)S(1)}, f32[32]{0:T(128)S(1)}, bf16[4,512,256]{2,1,0:T(8,128)(2,1)}, bf16[32,256]{1,0:T(8,128)(2,1)S(1)}, ...), condition=%wide.region_7.8_spmd.clone, body=%wide.region_4.7_spmd.clone.sunk | while | flops 8437923 | bytes 411864 | solution.py:61
  100.7 1.2 fusion.50
  102.2 1.2 fusion.50
  103.7 1.2 fusion.50
  105.2 1.2 fusion.50
  107.2 37.0 %all-reduce.2 = (f32[1024]{0:T(1024)S(1)}, f32[1024]{0:T(1024)S(1)}) all-reduce(f32[1024]{0:T(1024)S(1)} %dynamic-update-slice, f32[1024]{0:T(1024)S(1)} %dynamic-update-slice.1), channel_id=2, replica_groups=mesh['dp'=4,'item'=8] {'dp','item'}, use_global_device_ids=true, to_apply=%add | all-reduce | flops 2048 | bytes 16384
  149.4 6.0 %all-to-all-start.3 = ((bf16[8,4,1,48,256]{4,3,1,2,0:T(8,128)(2,1)}), bf16[8,4,1,48,256]{4,3,1,2,0:T(8,128)(2,1)S(1)}, u32[]{:S(2)}, u32[]{:S(2)}) async-start(bf16[8,4,1,48,256]{4,3,1,2,0:T(8,128)(2,1)} %fusion.17), calls=%async_computation.3 | async-start | bytes 1572864 | tf_op jit(solution)/shard_map/all_to_all | solution.py:84
  155.4 1.4 while.30
  159.6 15.6 %all-to-all-done.3 = bf16[8,4,1,48,256]{4,3,1,2,0:T(8,128)(2,1)S(1)} async-done(((bf16[8,4,1,48,256]{4,3,1,2,0:T(8,128)(2,1)}), bf16[8,4,1,48,256]{4,3,1,2,0:T(8,128)(2,1)S(1)}, u32[]{:S(2)}, u32[]{:S(2)}) %all-to-all-start.3) | async-done | bytes 786464 | tf_op jit(solution)/shard_map/all_to_all | solution.py:84
  175.3 3.9 %gather_fusion.1 = bf16[1024,256]{1,0:T(8,128)(2,1)S(1)} fusion(bf16[1536,256]{1,0:T(8,128)(2,1)S(1)} %bitcast.121, s32[1024]{0:T(1024)S(1)} %broadcast_clamp_fusion), kind=kCustom, calls=%fused_computation.1 | custom fusion | bytes 1052672 | tf_op jit(solution)/shard_map/gather | solution.py:100
  179.5 1.4 multiply_convert_fusion
  181.9 1.3 select_reduce_fusion.1
  184.6 1.9 %select_reduce_fusion = (f32[]{:T(128)}, f32[1024]{0:T(1024)}) fusion(s32[]{:T(128)} %bitcast.119, f32[]{:T(128)} %bitcast.24, f32[1024]{0:T(1024)S(1)} %bitcast.130, f32[1024]{0:T(1024)S(1)} %bitcast.126, f32[]{:T(128)S(6)} %add.144, s32[]{:T(128)} %bitcast.118), kind=kLoop, calls=%fused_computation.64 | loop fusion | flops 9215 | bytes 12308 | tf_op jit(solution)/shard_map/reduce_sum | solution.py:132
  (99 shorter events, 11.7 us)
Async XLA Ops:
  0.6 178.9 %copy-start = (bf16[512,512]{1,0:T(8,128)(2,1)S(1)}, bf16[512,512]{1,0:T(8,128)(2,1)}, u32[]{:S(2)}) copy-start(bf16[512,512]{1,0:T(8,128)(2,1)} %param.22) | copy-start | bytes 1572868
  17.8 72.6 %all-to-all-start.1 = ((s32[8,1,192]{2,1,0:T(1,128)}), s32[8,1,192]{2,1,0:T(1,128)S(1)}, u32[]{:S(2)}, u32[]{:S(2)}) async-start(s32[8,1,192]{2,1,0:T(1,128)} %reshape.236), calls=%async_computation.1 | async-start | bytes 16384 | tf_op jit(solution)/shard_map/all_to_all | solution.py:75
  97.2 47.1 %all-to-all-start.2 = ((bf16[4,8,48,256]{3,2,1,0:T(8,128)(2,1)}), bf16[4,8,48,256]{3,2,1,0:T(8,128)(2,1)S(1)}, u32[]{:S(2)}, u32[]{:S(2)}) async-start(bf16[4,8,48,256]{3,2,1,0:T(8,128)(2,1)} %bitcast.8), calls=%async_computation.2 | async-start | bytes 1572864 | tf_op jit(solution)/shard_map/all_to_all | solution.py:87
  148.8 8.0 %copy-start.4 = (bf16[512]{0:T(512)(128)(2,1)S(1)}, bf16[512]{0:T(512)(128)(2,1)}, u32[]{:S(2)}) copy-start(bf16[512]{0:T(512)(128)(2,1)} %param.23) | copy-start | bytes 3076
  148.8 10.7 %copy-start.1 = (bf16[768,512]{1,0:T(8,128)(2,1)S(1)}, bf16[768,512]{1,0:T(8,128)(2,1)}, u32[]{:S(2)}) copy-start(bf16[768,512]{1,0:T(8,128)(2,1)} %param.21) | copy-start | bytes 2359300
  148.8 10.7 %copy-start.3 = (bf16[1,512]{1,0:T(2,128)(2,1)S(1)}, bf16[1,512]{1,0:T(2,128)(2,1)}, u32[]{:S(2)}) copy-start(bf16[1,512]{1,0:T(2,128)(2,1)} %param.16) | copy-start | bytes 3076
  149.4 25.8 %all-to-all-start.3 = ((bf16[8,4,1,48,256]{4,3,1,2,0:T(8,128)(2,1)}), bf16[8,4,1,48,256]{4,3,1,2,0:T(8,128)(2,1)S(1)}, u32[]{:S(2)}, u32[]{:S(2)}) async-start(bf16[8,4,1,48,256]{4,3,1,2,0:T(8,128)(2,1)} %fusion.17), calls=%async_computation.3 | async-start | bytes 1572864 | tf_op jit(solution)/shard_map/all_to_all | solution.py:84
  175.3 4.0 %copy-start.2 = (bf16[1,256]{1,0:T(2,128)(2,1)S(1)}, bf16[1,256]{1,0:T(2,128)(2,1)}, u32[]{:S(2)}) copy-start(bf16[1,256]{1,0:T(2,128)(2,1)} %param.14) | copy-start | bytes 1540
